TPU v7x, 256 devices: a whole 4x4x8 slice. The times are simulated.
256 devices in a mesh: space: 32 (over z_hi, x, core), tm: 8 (over z_lo, y).
Axes of the slice: x: 4, y: 4, z: 8 (z_hi: 4, z_lo: 2; z = z_hi * 2 + z_lo), core: 2. Of those that a mesh axis runs over, the one named last changes fastest.
Arguments:
- start_state: float32 [1024, 8192], P('space'), may hold values from -6 to 6
- old_starts: float32 [8, 1024, 8192], P('tm', 'space'), may hold values from -6 to 6
- conductivity: float32 [1024, 8192], P('space'), may hold values from 0.1 to 0.7
- velocity: float32 [2, 1024, 8192], P(None, 'space'), may hold values from -0.2 to 0.2
- coarse_gain: float32 [8, 1024, 8192], P('tm', 'space'), may hold values from 0.4 to 0.99
- targets: float32 [8, 1024, 8192], P('tm', 'space'), may hold values from -6 to 6
Outputs:
- new_ends: float32 [8, 1024, 8192], P('tm', 'space')
- gradient: float32 [1024, 8192], P('space')
All inputs are finite; a program needn't handle non-finite values.
Results may differ from a plain program's by a relative error of at most 0.00002.
Values sent between devices are 32-bit elements; how exact they have to be, the bound alone decides.
A program may use at most 128 MiB of HBM per device.

v0:
```python
import jax
import jax.numpy as jnp
from jax import lax
from jax.sharding import PartitionSpec as P

STEPS = 4
HALO = 8
time_step = 0.25


def with_halo(cells, axis, dim):
    count = lax.axis_size(axis)
    ends = count - 1
    head = lax.slice_in_dim(cells, 0, 1, axis=dim)
    tail = lax.slice_in_dim(cells, cells.shape[dim] - 1, cells.shape[dim], axis=dim)
    return jnp.concatenate(
        [
            lax.ppermute(tail, axis, [(i, (i + 1) % count) for i in range(ends)]),
            cells,
            lax.ppermute(head, axis, [((i + 1) % count, i) for i in range(ends)]),
        ],
        axis=dim,
    )


def potential(field):
    return field + 0.25 * jnp.tanh(field)


def advance(padded, kappa, along_rows, along_cols):
    wide = jnp.pad(padded, ((0, 0), (0, 0), (1, 1)))
    shaped = potential(wide)
    centre = wide[:, 1:-1, 1:-1]
    spread = (
        shaped[:, :-2, 1:-1]
        + shaped[:, 2:, 1:-1]
        + shaped[:, 1:-1, :-2]
        + shaped[:, 1:-1, 2:]
        - 4.0 * shaped[:, 1:-1, 1:-1]
    )
    transport = (
        jnp.maximum(along_rows, 0.0) * (centre - wide[:, :-2, 1:-1])
        + jnp.minimum(along_rows, 0.0) * (wide[:, 2:, 1:-1] - centre)
        + jnp.maximum(along_cols, 0.0) * (centre - wide[:, 1:-1, :-2])
        + jnp.minimum(along_cols, 0.0) * (wide[:, 1:-1, 2:] - centre)
    )
    return centre + time_step * (kappa * spread - transport)


def fine(field, kappa, along_rows, along_cols, inside):
    for step in range(STEPS):
        padded = with_halo(field, "space", 1)
        field = jnp.where(inside, advance(padded, kappa, along_rows, along_cols), 0.0)
    return field


def pad_cols(x):
    return jnp.pad(x, [(0, 0)] * (x.ndim - 1) + [(HALO, HALO)])


def own_window(x, start, width):
    return lax.dynamic_slice_in_dim(pad_cols(x), start, width, axis=x.ndim - 1)


def on_device(start_state, old_starts, conductivity, velocity, coarse_gain, targets):
    blocks = lax.axis_size("tm")
    block = lax.axis_index("tm")
    rows, cols = start_state.shape
    width = cols // blocks
    wide = width + 2 * HALO

    def send_windows(x):
        padded = pad_cols(x)
        return jnp.stack([padded[:, k * width : k * width + wide] for k in range(blocks)])

    def to_blocks(x):
        return lax.all_to_all(send_windows(x), "tm", 0, 0, tiled=True)

    old = to_blocks(old_starts[0])
    gain = to_blocks(coarse_gain[0])
    target = to_blocks(targets[0])
    first = block * width
    kappa = own_window(conductivity, first, wide)
    flow = own_window(velocity, first, wide)
    begin = own_window(start_state, first, wide)
    column = first - HALO + lax.broadcasted_iota(jnp.int32, (1, 1, wide), 2)
    inside = (column >= 0) & (column < cols)
    fine_ends, pullback = jax.vjp(lambda k: fine(old, k, flow[0], flow[1], inside), kappa)
    carried = fine_ends - gain * old
    ends = []
    for slab in range(blocks):
        begin = gain[slab] * begin + carried[slab]
        ends.append(begin)
    new_ends = jnp.stack(ends)
    misfit = new_ends - target
    adjoints = [misfit[blocks - 1]]
    for slab in range(blocks - 2, -1, -1):
        adjoints.insert(0, misfit[slab] + gain[slab + 1] * adjoints[0])
    adjoint = jnp.stack(adjoints)
    (grad_window,) = pullback(adjoint)
    interior = new_ends[:, :, HALO : HALO + width]
    new_end = lax.all_to_all(interior, "tm", 0, 2, tiled=True)
    gradient = lax.all_gather(grad_window[:, HALO : HALO + width], "tm", axis=1, tiled=True)
    return (new_end, gradient)


def solution(mesh):
    in_specs = (
        P("space", None),
        P("tm", "space", None),
        P("space", None),
        P(None, "space", None),
        P("tm", "space", None),
        P("tm", "space", None),
    )
    out_specs = (P("tm", "space", None), P("space", None))
    return jax.shard_map(
        on_device, mesh=mesh, in_specs=in_specs, out_specs=out_specs, check_vma=False
    )
```

profile of v0, /device:TPU:2, one launch (start us, length us, event | category | flops | bytes accessed | tf_op | source)
XLA Modules:
  0.0 241.2 jit_solution(3339310915675040073)
XLA Ops:
  14.3 6.0 %all-to-all-start.1 = ((f32[8,32,1040]{2,1,0:T(8,128)}), f32[8,32,1040]{2,1,0:T(8,128)S(1)}, u32[]{:S(2)}, u32[]{:S(2)}) async-start(f32[8,32,1040]{2,1,0:T(8,128)} %fusion.80), calls=%async_computation.1 | async-start | bytes 2359296 | tf_op jit(solution)/shard_map/all_to_all | solution.py:77
  32.8 3.6 %all-to-all-done.1 = f32[8,32,1040]{2,1,0:T(8,128)S(1)} async-done(((f32[8,32,1040]{2,1,0:T(8,128)}), f32[8,32,1040]{2,1,0:T(8,128)S(1)}, u32[]{:S(2)}, u32[]{:S(2)}) %all-to-all-start.1) | async-done | bytes 1064992 | tf_op jit(solution)/shard_map/all_to_all | solution.py:77
  36.5 3.6 %all-to-all-start = ((f32[8,32,1040]{2,1,0:T(8,128)}), f32[8,32,1040]{2,1,0:T(8,128)S(1)}, u32[]{:S(2)}, u32[]{:S(2)}) async-start(f32[8,32,1040]{2,1,0:T(8,128)} %fusion.76), calls=%async_computation | async-start | bytes 2359296 | tf_op jit(solution)/shard_map/all_to_all | solution.py:77
  42.1 3.6 %collective-permute-start.1 = (f32[8,1,1040]{2,1,0:T(1,128)S(1)}, f32[8,1,1040]{2,1,0:T(1,128)S(1)}, u32[]{:S(2)}, u32[]{:S(2)}) collective-permute-start(f32[8,1,1040]{2,1,0:T(1,128)S(1)} %get-tuple-element.76), channel_id=1, source_target_pairs={{8,0},{16,8},{24,16},{32,24},{40,32},{48,40},{56,48},{64,56},{72,6... | collective-permute-start | bytes 99848 | tf_op jit(solution)/shard_map/jvp()/ppermute | solution.py:20
  48.0 3.0 %fusion.58 = (f32[8,32,1040]{2,1,0:T(8,128)S(1)}, f32[8,32,1040]{2,1,0:T(8,128)}) fusion(f32[8,32,1040]{2,1,0:T(8,128)S(1)} %all-to-all-done.1, f32[8,34,1042]{2,1,0:T(8,128)S(1)} %get-tuple-element.66, f32[8,1,1040]{2,1,0:T(1,128)S(1)} %collective-permute-done.1, f32[8,1,1040]{2,1,0:T(1,128)S(1)} %collective-permute-done, ...), kind=kLoop, calls=%fused_computation.105 | loop fusion | flops 6123520 | bytes 11382800 | tf_op jit(solution)/shard_map/jvp(jit(_where))/select_n | solution.py:53
  51.1 3.8 %collective-permute-start.2 = (f32[8,1,1040]{2,1,0:T(1,128)S(1)}, f32[8,1,1040]{2,1,0:T(1,128)S(1)}, u32[]{:S(2)}, u32[]{:S(2)}) collective-permute-start(f32[8,1,1040]{2,1,0:T(1,128)S(1)} %get-tuple-element.73), channel_id=1, source_target_pairs={{0,8},{8,16},{16,24},{24,32},{32,40},{40,48},{48,56},{56,64},{64,7... | collective-permute-start | bytes 99848 | tf_op jit(solution)/shard_map/jvp()/ppermute | solution.py:18
  59.3 3.0 %fusion.44 = (f32[8,32,1040]{2,1,0:T(8,128)S(1)}, f32[8,32,1040]{2,1,0:T(8,128)}) fusion(f32[8,32,1040]{2,1,0:T(8,128)S(1)} %get-tuple-element.32, f32[8,34,1042]{2,1,0:T(8,128)S(1)} %get-tuple-element.64, f32[8,1,1040]{2,1,0:T(1,128)S(1)} %collective-permute-done.3, f32[8,1,1040]{2,1,0:T(1,128)S(1)} %collective-permute-done.2, ...), kind=kLoop, calls=%fused_computation.83 | loop fusion | flops 6123520 | bytes 11382800 | tf_op jit(solution)/shard_map/jvp(jit(_where))/select_n | solution.py:53
  62.3 3.5 %collective-permute-start.4 = (f32[8,1,1040]{2,1,0:T(1,128)S(1)}, f32[8,1,1040]{2,1,0:T(1,128)S(1)}, u32[]{:S(2)}, u32[]{:S(2)}) collective-permute-start(f32[8,1,1040]{2,1,0:T(1,128)S(1)} %get-tuple-element.71), channel_id=1, source_target_pairs={{0,8},{8,16},{16,24},{24,32},{32,40},{40,48},{48,56},{56,64},{64,7... | collective-permute-start | bytes 99848 | tf_op jit(solution)/shard_map/jvp()/ppermute | solution.py:18
  70.2 3.0 %fusion.30 = (f32[8,32,1040]{2,1,0:T(8,128)S(1)}, f32[8,32,1040]{2,1,0:T(8,128)}) fusion(f32[8,32,1040]{2,1,0:T(8,128)S(1)} %get-tuple-element.30, f32[8,34,1042]{2,1,0:T(8,128)S(1)} %get-tuple-element.62, f32[8,1,1040]{2,1,0:T(1,128)S(1)} %collective-permute-done.5, f32[8,1,1040]{2,1,0:T(1,128)S(1)} %collective-permute-done.4, ...), kind=kLoop, calls=%fused_computation.61 | loop fusion | flops 6123520 | bytes 11382800 | tf_op jit(solution)/shard_map/jvp(jit(_where))/select_n | solution.py:53
  73.3 7.5 %collective-permute-start.6 = (f32[8,1,1040]{2,1,0:T(1,128)S(1)}, f32[8,1,1040]{2,1,0:T(1,128)S(1)}, u32[]{:S(2)}, u32[]{:S(2)}) collective-permute-start(f32[8,1,1040]{2,1,0:T(1,128)S(1)} %get-tuple-element.69), channel_id=1, source_target_pairs={{0,8},{8,16},{16,24},{24,32},{32,40},{40,48},{48,56},{56,64},{64,7... | collective-permute-start | bytes 99848 | tf_op jit(solution)/shard_map/jvp()/ppermute | solution.py:18
  83.4 2.9 %collective-permute-done.7 = f32[8,1,1040]{2,1,0:T(1,128)S(1)} collective-permute-done((f32[8,1,1040]{2,1,0:T(1,128)S(1)}, f32[8,1,1040]{2,1,0:T(1,128)S(1)}, u32[]{:S(2)}, u32[]{:S(2)}) %collective-permute-start.7) | collective-permute-done | bytes 33312 | tf_op jit(solution)/shard_map/jvp()/ppermute | solution.py:20
  88.7 7.3 %all-to-all-start.3 = ((f32[8,32,1040]{2,1,0:T(8,128)}), f32[8,32,1040]{2,1,0:T(8,128)}, u32[]{:S(2)}, u32[]{:S(2)}) async-start(f32[8,32,1040]{2,1,0:T(8,128)} %fusion.84), calls=%async_computation.3 | async-start | bytes 2359296 | tf_op jit(solution)/shard_map/all_to_all | solution.py:77
  96.0 6.1 %fusion.16 = (f32[8,32,1040]{2,1,0:T(8,128)S(1)}, f32[8,32,1040]{2,1,0:T(8,128)}) fusion(f32[8,32,1040]{2,1,0:T(8,128)} %copy-done.4, f32[8,34,1042]{2,1,0:T(8,128)} %get-tuple-element.60, f32[8,1,1040]{2,1,0:T(1,128)} %copy-done.32, f32[8,1,1040]{2,1,0:T(1,128)} %copy-done.30, f32[8,32,1040]{2,1,0:T(8,128)S(1)} %all-to-all-done, ...), kind=kLoop, calls=%fused_computation.39 | loop fusion | flops 6656000 | bytes 13512720 | tf_op jit(solution)/shard_map/sub | solution.py:89
  102.5 6.3 %all-to-all-done.3 = f32[8,32,1040]{2,1,0:T(8,128)} async-done(((f32[8,32,1040]{2,1,0:T(8,128)}), f32[8,32,1040]{2,1,0:T(8,128)}, u32[]{:S(2)}, u32[]{:S(2)}) %all-to-all-start.3) | async-done | bytes 1064992 | tf_op jit(solution)/shard_map/all_to_all | solution.py:77
  112.2 4.6 %multiply_add_fusion.2 = f32[8,34,1042]{2,1,0:T(8,128)S(1)} fusion(f32[8,32,1040]{2,1,0:T(8,128)S(1)} %get-tuple-element.68, f32[8,32,1040]{2,1,0:T(8,128)S(1)} %get-tuple-element.67, f32[8,32,1040]{2,1,0:T(8,128)S(1)} %get-tuple-element.55, f32[8,32,1040]{2,1,0:T(8,128)S(1)} %get-tuple-element.56, f32[8,32,1040]{2,1,0:T(8,128)S(1)} %get-tuple-element.57, ...), kind=kLoop, calls=%fused_computation.14 | loop fusion | flops 6518752 | bytes 9719936 | tf_op jit(solution)/shard_map/transpose(jvp())/add_any | solution.py:27
  119.0 6.7 %collective-permute-start.9 = (f32[8,1,1040]{2,1,0:T(1,128)S(1)}, f32[8,1,1040]{2,1,0:T(1,128)S(1)}, u32[]{:S(2)}, u32[]{:S(2)}) collective-permute-start(f32[8,1,1040]{2,1,0:T(1,128)S(1)} %get-tuple-element.53), channel_id=1, source_target_pairs={{0,8},{8,16},{16,24},{24,32},{32,40},{40,48},{48,56},{56,64},{64,7... | collective-permute-start | bytes 99848 | tf_op jit(solution)/shard_map/transpose(jvp())/ppermute | solution.py:20
  128.4 4.6 %multiply_add_fusion.1 = f32[8,34,1042]{2,1,0:T(8,128)S(1)} fusion(f32[8,32,1040]{2,1,0:T(8,128)S(1)} %get-tuple-element.9, f32[8,32,1040]{2,1,0:T(8,128)S(1)} %get-tuple-element.8, f32[8,32,1040]{2,1,0:T(8,128)S(1)} %get-tuple-element.43, f32[8,32,1040]{2,1,0:T(8,128)S(1)} %get-tuple-element.44, f32[8,32,1040]{2,1,0:T(8,128)S(1)} %get-tuple-element.45, ...), kind=kLoop, calls=%fused_computation.13 | loop fusion | flops 6518752 | bytes 9719936 | tf_op jit(solution)/shard_map/transpose(jvp())/add_any | solution.py:27
  135.2 4.1 %collective-permute-start.11 = (f32[8,1,1040]{2,1,0:T(1,128)S(1)}, f32[8,1,1040]{2,1,0:T(1,128)S(1)}, u32[]{:S(2)}, u32[]{:S(2)}) collective-permute-start(f32[8,1,1040]{2,1,0:T(1,128)S(1)} %get-tuple-element.51), channel_id=1, source_target_pairs={{0,8},{8,16},{16,24},{24,32},{32,40},{40,48},{48,56},{56,64},{64,7... | collective-permute-start | bytes 99848 | tf_op jit(solution)/shard_map/transpose(jvp())/ppermute | solution.py:20
  142.3 4.6 %multiply_add_fusion = f32[8,34,1042]{2,1,0:T(8,128)S(1)} fusion(f32[8,32,1040]{2,1,0:T(8,128)S(1)} %get-tuple-element.7, f32[8,32,1040]{2,1,0:T(8,128)S(1)} %get-tuple-element.6, f32[8,32,1040]{2,1,0:T(8,128)S(1)} %get-tuple-element.39, f32[8,32,1040]{2,1,0:T(8,128)S(1)} %get-tuple-element.40, f32[8,32,1040]{2,1,0:T(8,128)S(1)} %get-tuple-element.41, ...), kind=kLoop, calls=%fused_computation.12 | loop fusion | flops 6518752 | bytes 9719936 | tf_op jit(solution)/shard_map/transpose(jvp())/add_any | solution.py:27
  150.3 4.5 %collective-permute-start.13 = (f32[8,1,1040]{2,1,0:T(1,128)S(1)}, f32[8,1,1040]{2,1,0:T(1,128)S(1)}, u32[]{:S(2)}, u32[]{:S(2)}) collective-permute-start(f32[8,1,1040]{2,1,0:T(1,128)S(1)} %get-tuple-element.49), channel_id=1, source_target_pairs={{0,8},{8,16},{16,24},{24,32},{32,40},{40,48},{48,56},{56,64},{64,7... | collective-permute-start | bytes 99848 | tf_op jit(solution)/shard_map/transpose(jvp())/ppermute | solution.py:20
  156.1 5.8 %all-to-all-start.2 = ((f32[8,32,1024]{2,1,0:T(8,128)}), f32[8,32,1024]{2,1,0:T(8,128)}, u32[]{:S(2)}, u32[]{:S(2)}) async-start(f32[8,32,1024]{2,1,0:T(8,128)} %slice.509), calls=%async_computation.2 | async-start | bytes 2097152 | tf_op jit(solution)/shard_map/all_to_all | solution.py:102
  162.5 4.6 %multiply_reduce_fusion.2 = (f32[32,1040]{1,0:T(8,128)S(1)}, f32[32,1040]{1,0:T(8,128)S(1)}, f32[32,1040]{1,0:T(8,128)S(1)}, f32[32,1040]{1,0:T(8,128)S(1)}) fusion(f32[8,32,1040]{2,1,0:T(8,128)} %get-tuple-element.27, f32[8,32,1040]{2,1,0:T(8,128)} %copy-done.11, pred[1040]{0:T(1024)(128)(4,1)S(1)} %fusion.117, f32[8,32,1040]{2,1,0:T(8,128)} %get-tuple-element.29, ...), kind=kLoop, calls=%fused_computation.129 | loop fusion | flops 5724160 | bytes 9252880 | tf_op jit(solution)/shard_map/transpose(jvp())/reduce_sum | solution.py:47
  168.0 9.7 %all-to-all-done.2 = f32[8,32,1024]{2,1,0:T(8,128)} async-done(((f32[8,32,1024]{2,1,0:T(8,128)}), f32[8,32,1024]{2,1,0:T(8,128)}, u32[]{:S(2)}, u32[]{:S(2)}) %all-to-all-start.2) | async-done | bytes 1048608 | tf_op jit(solution)/shard_map/all_to_all | solution.py:102
  180.1 52.0 %all-gather.2.cloned.1.call-done = f32[32,8192]{1,0:T(8,128)} async-done(((f32[32,1024]{1,0:T(8,128)}), f32[32,8192]{1,0:T(8,128)}) %all-gather.2.cloned.1.call-update) | async-done | bytes 1048592 | tf_op jit(solution)/shard_map/all_gather | solution.py:103
  (159 shorter events, 62.3 us)
Async XLA Ops:
  14.3 22.2 %all-to-all-start.1 = ((f32[8,32,1040]{2,1,0:T(8,128)}), f32[8,32,1040]{2,1,0:T(8,128)S(1)}, u32[]{:S(2)}, u32[]{:S(2)}) async-start(f32[8,32,1040]{2,1,0:T(8,128)} %fusion.80), calls=%async_computation.1 | async-start | bytes 2359296 | tf_op jit(solution)/shard_map/all_to_all | solution.py:77
  27.4 99.1 %copy-start.15 = (f32[32,1040]{1,0:T(8,128)}, f32[32,1040]{1,0:T(8,128)S(1)}, u32[]{:S(2)}) copy-start(f32[32,1040]{1,0:T(8,128)S(1)} %get-tuple-element.12) | copy-start | bytes 399364
  36.5 11.5 %copy-start.6 = (f32[8,32,1040]{2,1,0:T(8,128)}, f32[8,32,1040]{2,1,0:T(8,128)S(1)}, u32[]{:S(2)}) copy-start(f32[8,32,1040]{2,1,0:T(8,128)S(1)} %all-to-all-done.1) | copy-start | bytes 3194884
  36.5 52.3 %all-to-all-start = ((f32[8,32,1040]{2,1,0:T(8,128)}), f32[8,32,1040]{2,1,0:T(8,128)S(1)}, u32[]{:S(2)}, u32[]{:S(2)}) async-start(f32[8,32,1040]{2,1,0:T(8,128)} %fusion.76), calls=%async_computation | async-start | bytes 2359296 | tf_op jit(solution)/shard_map/all_to_all | solution.py:77
  40.1 5.6 %collective-permute-start = (f32[8,1,1040]{2,1,0:T(1,128)S(1)}, f32[8,1,1040]{2,1,0:T(1,128)S(1)}, u32[]{:S(2)}, u32[]{:S(2)}) collective-permute-start(f32[8,1,1040]{2,1,0:T(1,128)S(1)} %get-tuple-element.75), channel_id=1, source_target_pairs={{0,8},{8,16},{16,24},{24,32},{32,40},{40,48},{48,56},{56,64},{64,7... | collective-permute-start | bytes 99848 | tf_op jit(solution)/shard_map/jvp()/ppermute | solution.py:18
  42.1 5.3 %collective-permute-start.1 = (f32[8,1,1040]{2,1,0:T(1,128)S(1)}, f32[8,1,1040]{2,1,0:T(1,128)S(1)}, u32[]{:S(2)}, u32[]{:S(2)}) collective-permute-start(f32[8,1,1040]{2,1,0:T(1,128)S(1)} %get-tuple-element.76), channel_id=1, source_target_pairs={{8,0},{16,8},{24,16},{32,24},{40,32},{48,40},{56,48},{64,56},{72,6... | collective-permute-start | bytes 99848 | tf_op jit(solution)/shard_map/jvp()/ppermute | solution.py:20
  51.1 6.7 %collective-permute-start.2 = (f32[8,1,1040]{2,1,0:T(1,128)S(1)}, f32[8,1,1040]{2,1,0:T(1,128)S(1)}, u32[]{:S(2)}, u32[]{:S(2)}) collective-permute-start(f32[8,1,1040]{2,1,0:T(1,128)S(1)} %get-tuple-element.73), channel_id=1, source_target_pairs={{0,8},{8,16},{16,24},{24,32},{32,40},{40,48},{48,56},{56,64},{64,7... | collective-permute-start | bytes 99848 | tf_op jit(solution)/shard_map/jvp()/ppermute | solution.py:18
  54.9 3.7 %collective-permute-start.3 = (f32[8,1,1040]{2,1,0:T(1,128)S(1)}, f32[8,1,1040]{2,1,0:T(1,128)S(1)}, u32[]{:S(2)}, u32[]{:S(2)}) collective-permute-start(f32[8,1,1040]{2,1,0:T(1,128)S(1)} %get-tuple-element.74), channel_id=1, source_target_pairs={{8,0},{16,8},{24,16},{32,24},{40,32},{48,40},{56,48},{64,56},{72,6... | collective-permute-start | bytes 99848 | tf_op jit(solution)/shard_map/jvp()/ppermute | solution.py:20
  62.3 6.4 %collective-permute-start.4 = (f32[8,1,1040]{2,1,0:T(1,128)S(1)}, f32[8,1,1040]{2,1,0:T(1,128)S(1)}, u32[]{:S(2)}, u32[]{:S(2)}) collective-permute-start(f32[8,1,1040]{2,1,0:T(1,128)S(1)} %get-tuple-element.71), channel_id=1, source_target_pairs={{0,8},{8,16},{16,24},{24,32},{32,40},{40,48},{48,56},{56,64},{64,7... | collective-permute-start | bytes 99848 | tf_op jit(solution)/shard_map/jvp()/ppermute | solution.py:18
  65.8 3.7 %collective-permute-start.5 = (f32[8,1,1040]{2,1,0:T(1,128)S(1)}, f32[8,1,1040]{2,1,0:T(1,128)S(1)}, u32[]{:S(2)}, u32[]{:S(2)}) collective-permute-start(f32[8,1,1040]{2,1,0:T(1,128)S(1)} %get-tuple-element.72), channel_id=1, source_target_pairs={{8,0},{16,8},{24,16},{32,24},{40,32},{48,40},{56,48},{64,56},{72,6... | collective-permute-start | bytes 99848 | tf_op jit(solution)/shard_map/jvp()/ppermute | solution.py:20
  73.2 13.1 %copy-start.4 = (f32[8,32,1040]{2,1,0:T(8,128)}, f32[8,32,1040]{2,1,0:T(8,128)S(1)}, u32[]{:S(2)}) copy-start(f32[8,32,1040]{2,1,0:T(8,128)S(1)} %get-tuple-element.28) | copy-start | bytes 3194884
  73.3 10.2 %collective-permute-start.6 = (f32[8,1,1040]{2,1,0:T(1,128)S(1)}, f32[8,1,1040]{2,1,0:T(1,128)S(1)}, u32[]{:S(2)}, u32[]{:S(2)}) collective-permute-start(f32[8,1,1040]{2,1,0:T(1,128)S(1)} %get-tuple-element.69), channel_id=1, source_target_pairs={{0,8},{8,16},{16,24},{24,32},{32,40},{40,48},{48,56},{56,64},{64,7... | collective-permute-start | bytes 99848 | tf_op jit(solution)/shard_map/jvp()/ppermute | solution.py:18
  80.7 5.6 %collective-permute-start.7 = (f32[8,1,1040]{2,1,0:T(1,128)S(1)}, f32[8,1,1040]{2,1,0:T(1,128)S(1)}, u32[]{:S(2)}, u32[]{:S(2)}) collective-permute-start(f32[8,1,1040]{2,1,0:T(1,128)S(1)} %get-tuple-element.70), channel_id=1, source_target_pairs={{8,0},{16,8},{24,16},{32,24},{40,32},{48,40},{56,48},{64,56},{72,6... | collective-permute-start | bytes 99848 | tf_op jit(solution)/shard_map/jvp()/ppermute | solution.py:20
  88.7 20.0 %all-to-all-start.3 = ((f32[8,32,1040]{2,1,0:T(8,128)}), f32[8,32,1040]{2,1,0:T(8,128)}, u32[]{:S(2)}, u32[]{:S(2)}) async-start(f32[8,32,1040]{2,1,0:T(8,128)} %fusion.84), calls=%async_computation.3 | async-start | bytes 2359296 | tf_op jit(solution)/shard_map/all_to_all | solution.py:77
  117.1 8.6 %collective-permute-start.8 = (f32[8,1,1040]{2,1,0:T(1,128)S(1)}, f32[8,1,1040]{2,1,0:T(1,128)S(1)}, u32[]{:S(2)}, u32[]{:S(2)}) collective-permute-start(f32[8,1,1040]{2,1,0:T(1,128)S(1)} %get-tuple-element.52), channel_id=1, source_target_pairs={{8,0},{16,8},{24,16},{32,24},{40,32},{48,40},{56,48},{64,56},{72,6... | collective-permute-start | bytes 99848 | tf_op jit(solution)/shard_map/transpose(jvp())/ppermute | solution.py:18
  119.0 7.5 %collective-permute-start.9 = (f32[8,1,1040]{2,1,0:T(1,128)S(1)}, f32[8,1,1040]{2,1,0:T(1,128)S(1)}, u32[]{:S(2)}, u32[]{:S(2)}) collective-permute-start(f32[8,1,1040]{2,1,0:T(1,128)S(1)} %get-tuple-element.53), channel_id=1, source_target_pairs={{0,8},{8,16},{16,24},{24,32},{32,40},{40,48},{48,56},{56,64},{64,7... | collective-permute-start | bytes 99848 | tf_op jit(solution)/shard_map/transpose(jvp())/ppermute | solution.py:20
  128.4 12.0 %copy-start.16 = (f32[32,1040]{1,0:T(8,128)S(1)}, f32[32,1040]{1,0:T(8,128)}, u32[]{:S(2)}) copy-start(f32[32,1040]{1,0:T(8,128)} %copy-done.15) | copy-start | bytes 399364
  133.2 6.0 %collective-permute-start.10 = (f32[8,1,1040]{2,1,0:T(1,128)S(1)}, f32[8,1,1040]{2,1,0:T(1,128)S(1)}, u32[]{:S(2)}, u32[]{:S(2)}) collective-permute-start(f32[8,1,1040]{2,1,0:T(1,128)S(1)} %get-tuple-element.50), channel_id=1, source_target_pairs={{8,0},{16,8},{24,16},{32,24},{40,32},{48,40},{56,48},{64,56},{72,6... | collective-permute-start | bytes 99848 | tf_op jit(solution)/shard_map/transpose(jvp())/ppermute | solution.py:18
  135.2 5.3 %collective-permute-start.11 = (f32[8,1,1040]{2,1,0:T(1,128)S(1)}, f32[8,1,1040]{2,1,0:T(1,128)S(1)}, u32[]{:S(2)}, u32[]{:S(2)}) collective-permute-start(f32[8,1,1040]{2,1,0:T(1,128)S(1)} %get-tuple-element.51), channel_id=1, source_target_pairs={{0,8},{8,16},{16,24},{24,32},{32,40},{40,48},{48,56},{56,64},{64,7... | collective-permute-start | bytes 99848 | tf_op jit(solution)/shard_map/transpose(jvp())/ppermute | solution.py:20
  142.3 12.4 %copy-start.14 = (f32[8,32,1040]{2,1,0:T(8,128)S(1)}, f32[8,32,1040]{2,1,0:T(8,128)}, u32[]{:S(2)}) copy-start(f32[8,32,1040]{2,1,0:T(8,128)} %copy-done.13) | copy-start | bytes 3194884
  148.3 13.6 %collective-permute-start.12 = (f32[8,1,1040]{2,1,0:T(1,128)S(1)}, f32[8,1,1040]{2,1,0:T(1,128)S(1)}, u32[]{:S(2)}, u32[]{:S(2)}) collective-permute-start(f32[8,1,1040]{2,1,0:T(1,128)S(1)} %get-tuple-element.48), channel_id=1, source_target_pairs={{8,0},{16,8},{24,16},{32,24},{40,32},{48,40},{56,48},{64,56},{72,6... | collective-permute-start | bytes 99848 | tf_op jit(solution)/shard_map/transpose(jvp())/ppermute | solution.py:18
  150.3 11.7 %collective-permute-start.13 = (f32[8,1,1040]{2,1,0:T(1,128)S(1)}, f32[8,1,1040]{2,1,0:T(1,128)S(1)}, u32[]{:S(2)}, u32[]{:S(2)}) collective-permute-start(f32[8,1,1040]{2,1,0:T(1,128)S(1)} %get-tuple-element.49), channel_id=1, source_target_pairs={{0,8},{8,16},{16,24},{24,32},{32,40},{40,48},{48,56},{56,64},{64,7... | collective-permute-start | bytes 99848 | tf_op jit(solution)/shard_map/transpose(jvp())/ppermute | solution.py:20
  156.1 21.7 %all-to-all-start.2 = ((f32[8,32,1024]{2,1,0:T(8,128)}), f32[8,32,1024]{2,1,0:T(8,128)}, u32[]{:S(2)}, u32[]{:S(2)}) async-start(f32[8,32,1024]{2,1,0:T(8,128)} %slice.509), calls=%async_computation.2 | async-start | bytes 2097152 | tf_op jit(solution)/shard_map/all_to_all | solution.py:102
  161.9 70.3 %all-gather.2.cloned.1.call-start = ((), (), s32[]{:S(2)}) async-start(), calls=%async_computation.4 | async-start | bytes 1179648 | tf_op jit(solution)/shard_map/all_gather | solution.py:103
  (31 other events, 76.7 us)
Sparse Core Ops, SparseCore 0:
  168.2 63.9 all-gather.1
where the time goes:
time: 242 us; the launch traced here: 241 us
  waiting for transfers between devices  79.9 us (33%)
  starting transfers between devices  70 us (29%)
  other arithmetic  46.4 us (19%)
  local copies, waits for them, and re-layouts  30.3 us (13%)
  between operations  14.6 us (6%)
    all_gather x1, waiting for transfers between devices, on_device(): lax.all_gather(grad_window[:, HALO:HALO + width], 'tm', axis=1, tiled=True)  52 us
    ppermute x7, starting transfers between devices, with_halo(): lax.ppermute(head, axis, [((i + 1) % count, i) for i in range(ends)])  24.9 us
    unnamed x97, local copies, waits for them, and re-layouts  23.5 us
    ppermute x7, starting transfers between devices, with_halo(): lax.ppermute(tail, axis, [(i, (i + 1) % count) for i in range(ends)])  22.5 us
    all_to_all x3, starting transfers between devices, to_blocks(): return lax.all_to_all(send_windows(x), 'tm', 0, 0, tiled=True)  16.8 us
    add_any x3, other arithmetic, potential(): return field + 0.25 * jnp.tanh(field)  13.8 us
    all_to_all x3, waiting for transfers between devices, to_blocks(): return lax.all_to_all(send_windows(x), 'tm', 0, 0, tiled=True)  9.89 us
    all_to_all x1, waiting for transfers between devices, on_device(): new_end = lax.all_to_all(interior, 'tm', 0, 2, tiled=True)  9.73 us
  transfers between devices with their start and end apart: 19, of which 10 were waited for; matrix products, arithmetic and copies ran while one was open for 18% of the time, Pallas kernels for 0%

commit v1 on v0

--- a/solution.py
+++ b/solution.py
@@ -100,7 +100,12 @@
     (grad_window,) = pullback(adjoint)
     interior = new_ends[:, :, HALO : HALO + width]
     new_end = lax.all_to_all(interior, "tm", 0, 2, tiled=True)
-    gradient = lax.all_gather(grad_window[:, HALO : HALO + width], "tm", axis=1, tiled=True)
+    gradient = jnp.concatenate(
+        lax.all_to_all(
+            jnp.stack([grad_window[:, HALO : HALO + width]] * lax.axis_size("tm")), "tm", 0, 0
+        ),
+        axis=1,
+    )
     return (new_end, gradient)
 
 

time: 242 us -> 204 us (0.84)
  the two profiles are of different devices: /device:TPU:2 before, /device:TPU:160 now
where the time goes in v1:
time: 204 us; the launch traced here: 202 us
  starting transfers between devices  88.2 us (43%)
  other arithmetic  45.3 us (22%)
  waiting for transfers between devices  39.1 us (19%)
  local copies, waits for them, and re-layouts  28.5 us (14%)
    ppermute x7, starting transfers between devices, with_halo(): lax.ppermute(head, axis, [((i + 1) % count, i) for i in range(ends)])  37.9 us
    ppermute x7, waiting for transfers between devices, with_halo(): lax.ppermute(head, axis, [((i + 1) % count, i) for i in range(ends)])  23.9 us
    ppermute x7, starting transfers between devices, with_halo(): lax.ppermute(tail, axis, [(i, (i + 1) % count) for i in range(ends)])  23.1 us
    unnamed x98, local copies, waits for them, and re-layouts  19 us
    all_to_all x3, starting transfers between devices, to_blocks(): return lax.all_to_all(send_windows(x), 'tm', 0, 0, tiled=True)  17.2 us
    add_any x3, other arithmetic, potential(): return field + 0.25 * jnp.tanh(field)  13.8 us
    select_n x3, other arithmetic, fine(): jnp.where(inside, advance(padded, kappa, along_rows, along_cols), 0.0)  8.96 us
    all_to_all x1, waiting for transfers between devices, on_device(): lax.all_to_all(jnp.stack([grad_window[:, HALO:HALO + width]] * lax.axis_s...  7.73 us
  transfers between devices with their start and end apart: 19, of which 10 were waited for; matrix products, arithmetic and copies ran while one was open for 24% of the time, Pallas kernels for 0%

profile of v1, /device:TPU:160, one launch (start us, length us, event | category | flops | bytes accessed | tf_op | source)
XLA Modules:
  0.0 202.4 jit_solution(6618003697688310424)
XLA Ops:
  7.8 6.1 %all-to-all-start.1 = ((f32[8,32,1040]{2,1,0:T(8,128)}), f32[8,32,1040]{2,1,0:T(8,128)S(1)}, u32[]{:S(2)}, u32[]{:S(2)}) async-start(f32[8,32,1040]{2,1,0:T(8,128)} %fusion.80), calls=%async_computation.1 | async-start | bytes 2359296 | tf_op jit(solution)/shard_map/all_to_all | solution.py:77
  26.4 3.1 %all-to-all-done.1 = f32[8,32,1040]{2,1,0:T(8,128)S(1)} async-done(((f32[8,32,1040]{2,1,0:T(8,128)}), f32[8,32,1040]{2,1,0:T(8,128)S(1)}, u32[]{:S(2)}, u32[]{:S(2)}) %all-to-all-start.1) | async-done | bytes 1064992 | tf_op jit(solution)/shard_map/all_to_all | solution.py:77
  29.5 4.2 %all-to-all-start = ((f32[8,32,1040]{2,1,0:T(8,128)}), f32[8,32,1040]{2,1,0:T(8,128)S(1)}, u32[]{:S(2)}, u32[]{:S(2)}) async-start(f32[8,32,1040]{2,1,0:T(8,128)} %fusion.76), calls=%async_computation | async-start | bytes 2359296 | tf_op jit(solution)/shard_map/all_to_all | solution.py:77
  35.6 7.9 %collective-permute-start.1 = (f32[8,1,1040]{2,1,0:T(1,128)S(1)}, f32[8,1,1040]{2,1,0:T(1,128)S(1)}, u32[]{:S(2)}, u32[]{:S(2)}) collective-permute-start(f32[8,1,1040]{2,1,0:T(1,128)S(1)} %get-tuple-element.76), channel_id=1, source_target_pairs={{8,0},{16,8},{24,16},{32,24},{40,32},{48,40},{56,48},{64,56},{72,6... | collective-permute-start | bytes 99848 | tf_op jit(solution)/shard_map/jvp()/ppermute | solution.py:20
  43.5 3.7 %collective-permute-done.1 = f32[8,1,1040]{2,1,0:T(1,128)S(1)} collective-permute-done((f32[8,1,1040]{2,1,0:T(1,128)S(1)}, f32[8,1,1040]{2,1,0:T(1,128)S(1)}, u32[]{:S(2)}, u32[]{:S(2)}) %collective-permute-start.1) | collective-permute-done | bytes 33312 | tf_op jit(solution)/shard_map/jvp()/ppermute | solution.py:20
  47.9 3.0 %fusion.58 = (f32[8,32,1040]{2,1,0:T(8,128)S(1)}, f32[8,32,1040]{2,1,0:T(8,128)}) fusion(f32[8,32,1040]{2,1,0:T(8,128)S(1)} %all-to-all-done.1, f32[8,34,1042]{2,1,0:T(8,128)S(1)} %get-tuple-element.66, f32[8,1,1040]{2,1,0:T(1,128)S(1)} %collective-permute-done.1, f32[8,1,1040]{2,1,0:T(1,128)S(1)} %collective-permute-done, ...), kind=kLoop, calls=%fused_computation.105 | loop fusion | flops 6123520 | bytes 11382800 | tf_op jit(solution)/shard_map/jvp(jit(_where))/select_n | solution.py:53
  52.9 8.0 %collective-permute-start.3 = (f32[8,1,1040]{2,1,0:T(1,128)S(1)}, f32[8,1,1040]{2,1,0:T(1,128)S(1)}, u32[]{:S(2)}, u32[]{:S(2)}) collective-permute-start(f32[8,1,1040]{2,1,0:T(1,128)S(1)} %get-tuple-element.74), channel_id=1, source_target_pairs={{8,0},{16,8},{24,16},{32,24},{40,32},{48,40},{56,48},{64,56},{72,6... | collective-permute-start | bytes 99848 | tf_op jit(solution)/shard_map/jvp()/ppermute | solution.py:20
  63.3 3.0 %fusion.44 = (f32[8,32,1040]{2,1,0:T(8,128)S(1)}, f32[8,32,1040]{2,1,0:T(8,128)}) fusion(f32[8,32,1040]{2,1,0:T(8,128)S(1)} %get-tuple-element.32, f32[8,34,1042]{2,1,0:T(8,128)S(1)} %get-tuple-element.64, f32[8,1,1040]{2,1,0:T(1,128)S(1)} %collective-permute-done.3, f32[8,1,1040]{2,1,0:T(1,128)S(1)} %collective-permute-done.2, ...), kind=kLoop, calls=%fused_computation.83 | loop fusion | flops 6123520 | bytes 11382800 | tf_op jit(solution)/shard_map/jvp(jit(_where))/select_n | solution.py:53
  68.2 7.9 %collective-permute-start.5 = (f32[8,1,1040]{2,1,0:T(1,128)S(1)}, f32[8,1,1040]{2,1,0:T(1,128)S(1)}, u32[]{:S(2)}, u32[]{:S(2)}) collective-permute-start(f32[8,1,1040]{2,1,0:T(1,128)S(1)} %get-tuple-element.72), channel_id=1, source_target_pairs={{8,0},{16,8},{24,16},{32,24},{40,32},{48,40},{56,48},{64,56},{72,6... | collective-permute-start | bytes 99848 | tf_op jit(solution)/shard_map/jvp()/ppermute | solution.py:20
  78.4 3.0 %fusion.30 = (f32[8,32,1040]{2,1,0:T(8,128)S(1)}, f32[8,32,1040]{2,1,0:T(8,128)}) fusion(f32[8,32,1040]{2,1,0:T(8,128)S(1)} %get-tuple-element.30, f32[8,34,1042]{2,1,0:T(8,128)S(1)} %get-tuple-element.62, f32[8,1,1040]{2,1,0:T(1,128)S(1)} %collective-permute-done.5, f32[8,1,1040]{2,1,0:T(1,128)S(1)} %collective-permute-done.4, ...), kind=kLoop, calls=%fused_computation.61 | loop fusion | flops 6123520 | bytes 11382800 | tf_op jit(solution)/shard_map/jvp(jit(_where))/select_n | solution.py:53
  83.4 7.9 %collective-permute-start.7 = (f32[8,1,1040]{2,1,0:T(1,128)S(1)}, f32[8,1,1040]{2,1,0:T(1,128)S(1)}, u32[]{:S(2)}, u32[]{:S(2)}) collective-permute-start(f32[8,1,1040]{2,1,0:T(1,128)S(1)} %get-tuple-element.70), channel_id=1, source_target_pairs={{8,0},{16,8},{24,16},{32,24},{40,32},{48,40},{56,48},{64,56},{72,6... | collective-permute-start | bytes 99848 | tf_op jit(solution)/shard_map/jvp()/ppermute | solution.py:20
  95.3 7.0 %all-to-all-start.3 = ((f32[8,32,1040]{2,1,0:T(8,128)}), f32[8,32,1040]{2,1,0:T(8,128)}, u32[]{:S(2)}, u32[]{:S(2)}) async-start(f32[8,32,1040]{2,1,0:T(8,128)} %fusion.84), calls=%async_computation.3 | async-start | bytes 2359296 | tf_op jit(solution)/shard_map/all_to_all | solution.py:77
  102.3 6.0 %fusion.16 = (f32[8,32,1040]{2,1,0:T(8,128)S(1)}, f32[8,32,1040]{2,1,0:T(8,128)}) fusion(f32[8,32,1040]{2,1,0:T(8,128)} %copy-done.4, f32[8,34,1042]{2,1,0:T(8,128)} %get-tuple-element.60, f32[8,1,1040]{2,1,0:T(1,128)} %copy-done.35, f32[8,1,1040]{2,1,0:T(1,128)} %copy-done.33, f32[8,32,1040]{2,1,0:T(8,128)S(1)} %all-to-all-done, ...), kind=kLoop, calls=%fused_computation.39 | loop fusion | flops 6656000 | bytes 13512720 | tf_op jit(solution)/shard_map/sub | solution.py:89
  108.7 4.4 %all-to-all-done.3 = f32[8,32,1040]{2,1,0:T(8,128)} async-done(((f32[8,32,1040]{2,1,0:T(8,128)}), f32[8,32,1040]{2,1,0:T(8,128)}, u32[]{:S(2)}, u32[]{:S(2)}) %all-to-all-start.3) | async-done | bytes 1064992 | tf_op jit(solution)/shard_map/all_to_all | solution.py:77
  116.6 4.6 %multiply_add_fusion.2 = f32[8,34,1042]{2,1,0:T(8,128)S(1)} fusion(f32[8,32,1040]{2,1,0:T(8,128)S(1)} %get-tuple-element.68, f32[8,32,1040]{2,1,0:T(8,128)S(1)} %get-tuple-element.67, f32[8,32,1040]{2,1,0:T(8,128)S(1)} %get-tuple-element.55, f32[8,32,1040]{2,1,0:T(8,128)S(1)} %get-tuple-element.56, f32[8,32,1040]{2,1,0:T(8,128)S(1)} %get-tuple-element.57, ...), kind=kLoop, calls=%fused_computation.14 | loop fusion | flops 6518752 | bytes 9719936 | tf_op jit(solution)/shard_map/transpose(jvp())/add_any | solution.py:27
  121.4 8.0 %collective-permute-start.8 = (f32[8,1,1040]{2,1,0:T(1,128)S(1)}, f32[8,1,1040]{2,1,0:T(1,128)S(1)}, u32[]{:S(2)}, u32[]{:S(2)}) collective-permute-start(f32[8,1,1040]{2,1,0:T(1,128)S(1)} %get-tuple-element.52), channel_id=1, source_target_pairs={{8,0},{16,8},{24,16},{32,24},{40,32},{48,40},{56,48},{64,56},{72,6... | collective-permute-start | bytes 99848 | tf_op jit(solution)/shard_map/transpose(jvp())/ppermute | solution.py:18
  131.4 7.9 %collective-permute-done.9 = f32[8,1,1040]{2,1,0:T(1,128)S(1)} collective-permute-done((f32[8,1,1040]{2,1,0:T(1,128)S(1)}, f32[8,1,1040]{2,1,0:T(1,128)S(1)}, u32[]{:S(2)}, u32[]{:S(2)}) %collective-permute-start.9) | collective-permute-done | bytes 33312 | tf_op jit(solution)/shard_map/transpose(jvp())/ppermute | solution.py:20
  141.2 4.6 %multiply_add_fusion.1 = f32[8,34,1042]{2,1,0:T(8,128)S(1)} fusion(f32[8,32,1040]{2,1,0:T(8,128)S(1)} %get-tuple-element.9, f32[8,32,1040]{2,1,0:T(8,128)S(1)} %get-tuple-element.8, f32[8,32,1040]{2,1,0:T(8,128)S(1)} %get-tuple-element.43, f32[8,32,1040]{2,1,0:T(8,128)S(1)} %get-tuple-element.44, f32[8,32,1040]{2,1,0:T(8,128)S(1)} %get-tuple-element.45, ...), kind=kLoop, calls=%fused_computation.13 | loop fusion | flops 6518752 | bytes 9719936 | tf_op jit(solution)/shard_map/transpose(jvp())/add_any | solution.py:27
  152.4 4.4 %all-to-all-start.2 = ((f32[8,32,1024]{2,1,0:T(8,128)}), f32[8,32,1024]{2,1,0:T(8,128)}, u32[]{:S(2)}, u32[]{:S(2)}) async-start(f32[8,32,1024]{2,1,0:T(8,128)} %slice.509), calls=%async_computation.2 | async-start | bytes 2097152 | tf_op jit(solution)/shard_map/all_to_all | solution.py:102
  162.1 4.6 %multiply_add_fusion = f32[8,34,1042]{2,1,0:T(8,128)S(1)} fusion(f32[8,32,1040]{2,1,0:T(8,128)S(1)} %get-tuple-element.7, f32[8,32,1040]{2,1,0:T(8,128)S(1)} %get-tuple-element.6, f32[8,32,1040]{2,1,0:T(8,128)S(1)} %get-tuple-element.39, f32[8,32,1040]{2,1,0:T(8,128)S(1)} %get-tuple-element.40, f32[8,32,1040]{2,1,0:T(8,128)S(1)} %get-tuple-element.41, ...), kind=kLoop, calls=%fused_computation.12 | loop fusion | flops 6518752 | bytes 9719936 | tf_op jit(solution)/shard_map/transpose(jvp())/add_any | solution.py:27
  166.9 5.4 %collective-permute-start.12 = (f32[8,1,1040]{2,1,0:T(1,128)S(1)}, f32[8,1,1040]{2,1,0:T(1,128)S(1)}, u32[]{:S(2)}, u32[]{:S(2)}) collective-permute-start(f32[8,1,1040]{2,1,0:T(1,128)S(1)} %get-tuple-element.48), channel_id=1, source_target_pairs={{8,0},{16,8},{24,16},{32,24},{40,32},{48,40},{56,48},{64,56},{72,6... | collective-permute-start | bytes 99848 | tf_op jit(solution)/shard_map/transpose(jvp())/ppermute | solution.py:18
  174.3 7.7 %collective-permute-done.13 = f32[8,1,1040]{2,1,0:T(1,128)S(1)} collective-permute-done((f32[8,1,1040]{2,1,0:T(1,128)S(1)}, f32[8,1,1040]{2,1,0:T(1,128)S(1)}, u32[]{:S(2)}, u32[]{:S(2)}) %collective-permute-start.13) | collective-permute-done | bytes 33312 | tf_op jit(solution)/shard_map/transpose(jvp())/ppermute | solution.py:20
  185.7 5.6 %all-to-all-start.4 = ((f32[8,32,1024]{2,1,0:T(8,128)}), f32[8,32,1024]{2,1,0:T(8,128)S(1)}, u32[]{:S(2)}, u32[]{:S(2)}) async-start(f32[8,32,1024]{2,1,0:T(8,128)} %stack.166), calls=%async_computation.4 | async-start | bytes 2097152 | tf_op jit(solution)/shard_map/all_to_all | solution.py:104
  193.7 7.7 %all-to-all-done.4 = f32[8,32,1024]{2,1,0:T(8,128)S(1)} async-done(((f32[8,32,1024]{2,1,0:T(8,128)}), f32[8,32,1024]{2,1,0:T(8,128)S(1)}, u32[]{:S(2)}, u32[]{:S(2)}) %all-to-all-start.4) | async-done | bytes 1048608 | tf_op jit(solution)/shard_map/all_to_all | solution.py:104
  (161 shorter events, 65.4 us)
Async XLA Ops:
  7.8 21.7 %all-to-all-start.1 = ((f32[8,32,1040]{2,1,0:T(8,128)}), f32[8,32,1040]{2,1,0:T(8,128)S(1)}, u32[]{:S(2)}, u32[]{:S(2)}) async-start(f32[8,32,1040]{2,1,0:T(8,128)} %fusion.80), calls=%async_computation.1 | async-start | bytes 2359296 | tf_op jit(solution)/shard_map/all_to_all | solution.py:77
  21.0 118.4 %copy-start.19 = (f32[32,1040]{1,0:T(8,128)}, f32[32,1040]{1,0:T(8,128)S(1)}, u32[]{:S(2)}) copy-start(f32[32,1040]{1,0:T(8,128)S(1)} %get-tuple-element.12) | copy-start | bytes 399364
  29.5 65.8 %all-to-all-start = ((f32[8,32,1040]{2,1,0:T(8,128)}), f32[8,32,1040]{2,1,0:T(8,128)S(1)}, u32[]{:S(2)}, u32[]{:S(2)}) async-start(f32[8,32,1040]{2,1,0:T(8,128)} %fusion.76), calls=%async_computation | async-start | bytes 2359296 | tf_op jit(solution)/shard_map/all_to_all | solution.py:77
  33.7 9.8 %collective-permute-start = (f32[8,1,1040]{2,1,0:T(1,128)S(1)}, f32[8,1,1040]{2,1,0:T(1,128)S(1)}, u32[]{:S(2)}, u32[]{:S(2)}) collective-permute-start(f32[8,1,1040]{2,1,0:T(1,128)S(1)} %get-tuple-element.75), channel_id=1, source_target_pairs={{0,8},{8,16},{16,24},{24,32},{32,40},{40,48},{48,56},{56,64},{64,7... | collective-permute-start | bytes 99848 | tf_op jit(solution)/shard_map/jvp()/ppermute | solution.py:18
  35.6 11.6 %collective-permute-start.1 = (f32[8,1,1040]{2,1,0:T(1,128)S(1)}, f32[8,1,1040]{2,1,0:T(1,128)S(1)}, u32[]{:S(2)}, u32[]{:S(2)}) collective-permute-start(f32[8,1,1040]{2,1,0:T(1,128)S(1)} %get-tuple-element.76), channel_id=1, source_target_pairs={{8,0},{16,8},{24,16},{32,24},{40,32},{48,40},{56,48},{64,56},{72,6... | collective-permute-start | bytes 99848 | tf_op jit(solution)/shard_map/jvp()/ppermute | solution.py:20
  51.0 10.7 %collective-permute-start.2 = (f32[8,1,1040]{2,1,0:T(1,128)S(1)}, f32[8,1,1040]{2,1,0:T(1,128)S(1)}, u32[]{:S(2)}, u32[]{:S(2)}) collective-permute-start(f32[8,1,1040]{2,1,0:T(1,128)S(1)} %get-tuple-element.73), channel_id=1, source_target_pairs={{0,8},{8,16},{16,24},{24,32},{32,40},{40,48},{48,56},{56,64},{64,7... | collective-permute-start | bytes 99848 | tf_op jit(solution)/shard_map/jvp()/ppermute | solution.py:18
  52.9 9.7 %collective-permute-start.3 = (f32[8,1,1040]{2,1,0:T(1,128)S(1)}, f32[8,1,1040]{2,1,0:T(1,128)S(1)}, u32[]{:S(2)}, u32[]{:S(2)}) collective-permute-start(f32[8,1,1040]{2,1,0:T(1,128)S(1)} %get-tuple-element.74), channel_id=1, source_target_pairs={{8,0},{16,8},{24,16},{32,24},{40,32},{48,40},{56,48},{64,56},{72,6... | collective-permute-start | bytes 99848 | tf_op jit(solution)/shard_map/jvp()/ppermute | solution.py:20
  66.3 10.6 %collective-permute-start.4 = (f32[8,1,1040]{2,1,0:T(1,128)S(1)}, f32[8,1,1040]{2,1,0:T(1,128)S(1)}, u32[]{:S(2)}, u32[]{:S(2)}) collective-permute-start(f32[8,1,1040]{2,1,0:T(1,128)S(1)} %get-tuple-element.71), channel_id=1, source_target_pairs={{0,8},{8,16},{16,24},{24,32},{32,40},{40,48},{48,56},{56,64},{64,7... | collective-permute-start | bytes 99848 | tf_op jit(solution)/shard_map/jvp()/ppermute | solution.py:18
  68.2 9.5 %collective-permute-start.5 = (f32[8,1,1040]{2,1,0:T(1,128)S(1)}, f32[8,1,1040]{2,1,0:T(1,128)S(1)}, u32[]{:S(2)}, u32[]{:S(2)}) collective-permute-start(f32[8,1,1040]{2,1,0:T(1,128)S(1)} %get-tuple-element.72), channel_id=1, source_target_pairs={{8,0},{16,8},{24,16},{32,24},{40,32},{48,40},{56,48},{64,56},{72,6... | collective-permute-start | bytes 99848 | tf_op jit(solution)/shard_map/jvp()/ppermute | solution.py:20
  81.5 10.6 %collective-permute-start.6 = (f32[8,1,1040]{2,1,0:T(1,128)S(1)}, f32[8,1,1040]{2,1,0:T(1,128)S(1)}, u32[]{:S(2)}, u32[]{:S(2)}) collective-permute-start(f32[8,1,1040]{2,1,0:T(1,128)S(1)} %get-tuple-element.69), channel_id=1, source_target_pairs={{0,8},{8,16},{16,24},{24,32},{32,40},{40,48},{48,56},{56,64},{64,7... | collective-permute-start | bytes 99848 | tf_op jit(solution)/shard_map/jvp()/ppermute | solution.py:18
  83.4 9.5 %collective-permute-start.7 = (f32[8,1,1040]{2,1,0:T(1,128)S(1)}, f32[8,1,1040]{2,1,0:T(1,128)S(1)}, u32[]{:S(2)}, u32[]{:S(2)}) collective-permute-start(f32[8,1,1040]{2,1,0:T(1,128)S(1)} %get-tuple-element.70), channel_id=1, source_target_pairs={{8,0},{16,8},{24,16},{32,24},{40,32},{48,40},{56,48},{64,56},{72,6... | collective-permute-start | bytes 99848 | tf_op jit(solution)/shard_map/jvp()/ppermute | solution.py:20
  95.3 17.8 %all-to-all-start.3 = ((f32[8,32,1040]{2,1,0:T(8,128)}), f32[8,32,1040]{2,1,0:T(8,128)}, u32[]{:S(2)}, u32[]{:S(2)}) async-start(f32[8,32,1040]{2,1,0:T(8,128)} %fusion.84), calls=%async_computation.3 | async-start | bytes 2359296 | tf_op jit(solution)/shard_map/all_to_all | solution.py:77
  121.4 10.0 %collective-permute-start.8 = (f32[8,1,1040]{2,1,0:T(1,128)S(1)}, f32[8,1,1040]{2,1,0:T(1,128)S(1)}, u32[]{:S(2)}, u32[]{:S(2)}) collective-permute-start(f32[8,1,1040]{2,1,0:T(1,128)S(1)} %get-tuple-element.52), channel_id=1, source_target_pairs={{8,0},{16,8},{24,16},{32,24},{40,32},{48,40},{56,48},{64,56},{72,6... | collective-permute-start | bytes 99848 | tf_op jit(solution)/shard_map/transpose(jvp())/ppermute | solution.py:18
  129.5 9.9 %collective-permute-start.9 = (f32[8,1,1040]{2,1,0:T(1,128)S(1)}, f32[8,1,1040]{2,1,0:T(1,128)S(1)}, u32[]{:S(2)}, u32[]{:S(2)}) collective-permute-start(f32[8,1,1040]{2,1,0:T(1,128)S(1)} %get-tuple-element.53), channel_id=1, source_target_pairs={{0,8},{8,16},{16,24},{24,32},{32,40},{40,48},{48,56},{56,64},{64,7... | collective-permute-start | bytes 99848 | tf_op jit(solution)/shard_map/transpose(jvp())/ppermute | solution.py:20
  146.7 10.1 %collective-permute-start.10 = (f32[8,1,1040]{2,1,0:T(1,128)}, f32[8,1,1040]{2,1,0:T(1,128)}, u32[]{:S(2)}, u32[]{:S(2)}) collective-permute-start(f32[8,1,1040]{2,1,0:T(1,128)} %get-tuple-element.50), channel_id=1, source_target_pairs={{8,0},{16,8},{24,16},{32,24},{40,32},{48,40},{56,48},{64,56},{72,6... | collective-permute-start | bytes 99848 | tf_op jit(solution)/shard_map/transpose(jvp())/ppermute | solution.py:18
  148.6 10.1 %collective-permute-start.11 = (f32[8,1,1040]{2,1,0:T(1,128)}, f32[8,1,1040]{2,1,0:T(1,128)}, u32[]{:S(2)}, u32[]{:S(2)}) collective-permute-start(f32[8,1,1040]{2,1,0:T(1,128)} %get-tuple-element.51), channel_id=1, source_target_pairs={{0,8},{8,16},{16,24},{24,32},{32,40},{40,48},{48,56},{56,64},{64,7... | collective-permute-start | bytes 99848 | tf_op jit(solution)/shard_map/transpose(jvp())/ppermute | solution.py:20
  152.4 32.3 %all-to-all-start.2 = ((f32[8,32,1024]{2,1,0:T(8,128)}), f32[8,32,1024]{2,1,0:T(8,128)}, u32[]{:S(2)}, u32[]{:S(2)}) async-start(f32[8,32,1024]{2,1,0:T(8,128)} %slice.509), calls=%async_computation.2 | async-start | bytes 2097152 | tf_op jit(solution)/shard_map/all_to_all | solution.py:102
  162.0 20.0 %copy-start.12 = (f32[8,32,1040]{2,1,0:T(8,128)S(1)}, f32[8,32,1040]{2,1,0:T(8,128)}, u32[]{:S(2)}) copy-start(f32[8,32,1040]{2,1,0:T(8,128)} %copy-done.11) | copy-start | bytes 3194884
  162.0 20.0 %copy-start.15 = (f32[8,32,1040]{2,1,0:T(8,128)S(1)}, f32[8,32,1040]{2,1,0:T(8,128)}, u32[]{:S(2)}) copy-start(f32[8,32,1040]{2,1,0:T(8,128)} %get-tuple-element.33) | copy-start | bytes 3194884
  162.0 20.0 %copy-start.16 = (f32[8,32,1040]{2,1,0:T(8,128)S(1)}, f32[8,32,1040]{2,1,0:T(8,128)}, u32[]{:S(2)}) copy-start(f32[8,32,1040]{2,1,0:T(8,128)} %get-tuple-element.31) | copy-start | bytes 3194884
  162.0 20.0 %copy-start.17 = (f32[8,32,1040]{2,1,0:T(8,128)S(1)}, f32[8,32,1040]{2,1,0:T(8,128)}, u32[]{:S(2)}) copy-start(f32[8,32,1040]{2,1,0:T(8,128)} %get-tuple-element.29) | copy-start | bytes 3194884
  166.9 7.4 %collective-permute-start.12 = (f32[8,1,1040]{2,1,0:T(1,128)S(1)}, f32[8,1,1040]{2,1,0:T(1,128)S(1)}, u32[]{:S(2)}, u32[]{:S(2)}) collective-permute-start(f32[8,1,1040]{2,1,0:T(1,128)S(1)} %get-tuple-element.48), channel_id=1, source_target_pairs={{8,0},{16,8},{24,16},{32,24},{40,32},{48,40},{56,48},{64,56},{72,6... | collective-permute-start | bytes 99848 | tf_op jit(solution)/shard_map/transpose(jvp())/ppermute | solution.py:18
  172.3 9.7 %collective-permute-start.13 = (f32[8,1,1040]{2,1,0:T(1,128)S(1)}, f32[8,1,1040]{2,1,0:T(1,128)S(1)}, u32[]{:S(2)}, u32[]{:S(2)}) collective-permute-start(f32[8,1,1040]{2,1,0:T(1,128)S(1)} %get-tuple-element.49), channel_id=1, source_target_pairs={{0,8},{8,16},{16,24},{24,32},{32,40},{40,48},{48,56},{56,64},{64,7... | collective-permute-start | bytes 99848 | tf_op jit(solution)/shard_map/transpose(jvp())/ppermute | solution.py:20
  185.7 15.7 %all-to-all-start.4 = ((f32[8,32,1024]{2,1,0:T(8,128)}), f32[8,32,1024]{2,1,0:T(8,128)S(1)}, u32[]{:S(2)}, u32[]{:S(2)}) async-start(f32[8,32,1024]{2,1,0:T(8,128)} %stack.166), calls=%async_computation.4 | async-start | bytes 2097152 | tf_op jit(solution)/shard_map/all_to_all | solution.py:104
  (32 other events, 188.9 us)
